TPU v7x, 32 devices: a whole 2x2x4 slice. The times are simulated.
32 devices in a mesh: dp: 4 (over z), ctx: 8 (over y, x, core).
Axes of the slice: x: 2, y: 2, z: 4, core: 2. Of those that a mesh axis runs over, the one named last changes fastest.
Arguments:
- queries: bfloat16 [4, 4096, 1024], P('dp', 'ctx'), may hold values from -6 to 6
- key_vectors: bfloat16 [4, 4096, 1024], P('dp', 'ctx'), may hold values from -6 to 6
- value_vectors: bfloat16 [4, 4096, 1024], P('dp', 'ctx'), may hold values from -6 to 6
- out_grad: bfloat16 [4, 4096, 1024], P('dp', 'ctx'), may hold values from -6 to 6
- column_bias: float32 [8], replicated, may hold values from -1 to 2
- column_offsets: int32 [1], replicated, may hold values from 0 to 63
Outputs:
- attended: bfloat16 [4, 4096, 1024], P('dp', 'ctx')
- query_grad: bfloat16 [4, 4096, 1024], P('dp', 'ctx')
- key_grad: bfloat16 [4, 4096, 1024], P('dp', 'ctx')
- value_grad: bfloat16 [4, 4096, 1024], P('dp', 'ctx')
- bias_grad: float32 [8], replicated
All inputs are finite; a program needn't handle non-finite values.
Results may differ from a plain program's by a relative error of at most 0.005.
The roundings to bfloat16 on the way count: a program that leaves them out, or rounds other values in their place, can miss the bound.
Values may be sent and summed in bfloat16 or wider, within the bound.
A program may use at most 128 MiB of HBM per device.

v0:
```python
import jax
import jax.numpy as jnp
from jax import lax
from jax.sharding import PartitionSpec as P

HEADS = 8
HEAD_DIM = 128
LOCAL_BAND = 512
STRIDE = 4096
CB = 64
TOKENS_PER_SHARD = 512


def from_behind(value, axis, by):
    size = lax.axis_size(axis)
    pairs = [(i, i + by) for i in range(size) if 0 <= i + by < size]
    return lax.ppermute(value, axis, pairs)


def column_flags(positions, offsets):
    window = positions // STRIDE
    within = positions % STRIDE
    picks = window[:, None] == jnp.arange(offsets.shape[0], dtype=jnp.int32)[None, :]
    offset_at = jnp.sum(jnp.where(picks, offsets[None, :], 0), axis=1)
    return (positions >= 0) & (within // CB == offset_at)


def head_block(qh, kb, vb, kc, vc, doh, bias_h, band_ok, band_col, col_ok):
    scale = HEAD_DIM ** (-0.5)
    sb = (
        jnp.dot(qh, kb.T, preferred_element_type=jnp.float32) * scale
        + jnp.where(band_col, bias_h, 0.0)[None, :]
    )
    sc = jnp.dot(qh, kc.T, preferred_element_type=jnp.float32) * scale + bias_h
    sb = jnp.where(band_ok, sb, -jnp.inf)
    sc = jnp.where(col_ok, sc, -jnp.inf)
    top = jnp.maximum(jnp.max(sb, axis=1), jnp.max(sc, axis=1))
    pb = jnp.exp(sb - top[:, None])
    pc = jnp.exp(sc - top[:, None])
    total = jnp.sum(pb, axis=1) + jnp.sum(pc, axis=1)
    wb = pb / total[:, None]
    wc = pc / total[:, None]
    wb16 = wb.astype(jnp.bfloat16)
    wc16 = wc.astype(jnp.bfloat16)
    mixed = jnp.dot(wb16, vb, preferred_element_type=jnp.float32) + jnp.dot(
        wc16, vc, preferred_element_type=jnp.float32
    )
    oh = mixed.astype(jnp.bfloat16)
    delta = jnp.sum(doh.astype(jnp.float32) * oh.astype(jnp.float32), axis=1)
    dsb = wb * (jnp.dot(doh, vb.T, preferred_element_type=jnp.float32) - delta[:, None])
    dsc = wc * (jnp.dot(doh, vc.T, preferred_element_type=jnp.float32) - delta[:, None])
    dbias = jnp.sum(jnp.where(band_col[None, :], dsb, 0.0)) + jnp.sum(dsc)
    dsb16 = dsb.astype(jnp.bfloat16)
    dsc16 = dsc.astype(jnp.bfloat16)
    dq = (
        (
            jnp.dot(dsb16, kb, preferred_element_type=jnp.float32)
            + jnp.dot(dsc16, kc, preferred_element_type=jnp.float32)
        )
        * scale
    ).astype(jnp.bfloat16)
    dkb = jnp.dot(dsb16.T, qh, preferred_element_type=jnp.float32) * scale
    dvb = jnp.dot(wb16.T, doh, preferred_element_type=jnp.float32)
    dkc = jnp.dot(dsc16.T, qh, preferred_element_type=jnp.float32) * scale
    dvc = jnp.dot(wc16.T, doh, preferred_element_type=jnp.float32)
    return (oh, dq, dkb, dvb, dkc, dvc, dbias, top, total, delta)


def separate_heads(x):
    return x.reshape(x.shape[0], HEADS, HEAD_DIM).transpose(1, 0, 2)


def join_heads(x):
    return x.transpose(1, 0, 2).reshape(x.shape[1], HEADS * HEAD_DIM)


def per_device(queries, key_vectors, value_vectors, out_grad, column_bias, column_offsets):
    here = lax.axis_index("ctx")
    count = lax.axis_size("ctx")
    start_position = here * TOKENS_PER_SHARD
    width = queries.shape[2]
    query_rows = queries[0]
    key_rows = key_vectors[0]
    value_rows = value_vectors[0]
    grad_rows = out_grad[0]
    ncol = column_offsets.shape[0]
    block_starts = jnp.arange(ncol, dtype=jnp.int32) * STRIDE + column_offsets * CB
    colpos = jnp.repeat(block_starts, CB) + jnp.tile(jnp.arange(CB, dtype=jnp.int32), ncol)
    window = start_position // STRIDE
    own_start = window * STRIDE + column_offsets[window] * CB
    local = jnp.clip(own_start - start_position, 0, TOKENS_PER_SHARD - CB)
    piece_k = lax.dynamic_slice_in_dim(key_rows, local, CB, 0)
    piece_v = lax.dynamic_slice_in_dim(value_rows, local, CB, 0)
    pieces_k, pieces_v = (
        lax.all_gather(piece_k, "ctx", axis=0, tiled=True),
        lax.all_gather(piece_v, "ctx", axis=0, tiled=True),
    )
    owner = block_starts // TOKENS_PER_SHARD
    col_k = pieces_k.reshape(count, CB, width)[owner].reshape(ncol * CB, width)
    col_v = pieces_v.reshape(count, CB, width)[owner].reshape(ncol * CB, width)
    prev_k, prev_v = from_behind((key_rows, value_rows), "ctx", 1)
    band_k = jnp.concatenate([prev_k, key_rows], axis=0)
    band_v = jnp.concatenate([prev_v, value_rows], axis=0)
    qpos = start_position + jnp.arange(TOKENS_PER_SHARD, dtype=jnp.int32)
    kpos = start_position - LOCAL_BAND + jnp.arange(LOCAL_BAND + TOKENS_PER_SHARD, dtype=jnp.int32)
    gap = qpos[:, None] - kpos[None, :]
    band_ok = (kpos[None, :] >= 0) & (gap >= 0) & (gap < LOCAL_BAND)
    band_col = column_flags(kpos, column_offsets)
    col_ok = colpos[None, :] <= qpos[:, None] - LOCAL_BAND

    def per_head(items):
        return head_block(
            items[0],
            items[1],
            items[2],
            items[3],
            items[4],
            items[5],
            items[6],
            band_ok,
            band_col,
            col_ok,
        )

    results = lax.map(
        per_head,
        (
            separate_heads(query_rows),
            separate_heads(band_k),
            separate_heads(band_v),
            separate_heads(col_k),
            separate_heads(col_v),
            separate_heads(grad_rows),
            column_bias,
        ),
    )
    oh, dq, dkb, dvb, dkc, dvc, dbias, top, total, delta = results
    attended = join_heads(oh)
    query_grad = join_heads(dq)
    dk_band = join_heads(dkb)
    dv_band = join_heads(dvb)
    own_dk = dk_band[dk_band.shape[0] - TOKENS_PER_SHARD :]
    own_dv = dv_band[dv_band.shape[0] - TOKENS_PER_SHARD :]
    back_k, back_v = from_behind((dk_band[:LOCAL_BAND], dv_band[:LOCAL_BAND]), "ctx", -1)
    own_dk = own_dk.at[TOKENS_PER_SHARD - LOCAL_BAND :].add(back_k)
    own_dv = own_dv.at[TOKENS_PER_SHARD - LOCAL_BAND :].add(back_v)
    summed_k, summed_v = lax.psum((join_heads(dkc), join_heads(dvc)), "ctx")
    flags = column_flags(qpos, column_offsets)
    source = jnp.clip(qpos // STRIDE * CB + qpos % CB, 0, ncol * CB - 1)
    own_dk = own_dk + jnp.where(flags[:, None], summed_k[source], 0.0)
    own_dv = own_dv + jnp.where(flags[:, None], summed_v[source], 0.0)
    bias_grad = lax.psum(dbias, ("dp", "ctx"))
    return (
        attended[None],
        query_grad[None],
        own_dk.astype(jnp.bfloat16)[None],
        own_dv.astype(jnp.bfloat16)[None],
        bias_grad,
    )


def solution(mesh):
    placed = (
        P("dp", "ctx", None),
        P("dp", "ctx", None),
        P("dp", "ctx", None),
        P("dp", "ctx", None),
        P(),
        P(),
    )
    return jax.shard_map(
        per_device,
        mesh=mesh,
        in_specs=placed,
        out_specs=(
            P("dp", "ctx", None),
            P("dp", "ctx", None),
            P("dp", "ctx", None),
            P("dp", "ctx", None),
            P(),
        ),
        check_vma=False,
    )
```

profile of v0, /device:TPU:0, one launch (start us, length us, event | category | flops | bytes accessed | tf_op | source)
XLA Modules:
  0.0 354.4 jit_solution(14615889557479074196)
XLA Ops:
  12.8 3.3 collective-permute-start
  16.7 4.5 %collective-permute-start.1 = (bf16[512,1024]{0,1:T(8,128)(2,1)S(1)}, bf16[512,1024]{0,1:T(8,128)(2,1)}, u32[]{:S(2)}, u32[]{:S(2)}) collective-permute-start(bf16[512,1024]{0,1:T(8,128)(2,1)S(1)} %bitcast.242), channel_id=1, source_target_pairs={{0,1},{1,2},{2,3},{3,4},{4,5},{5,6},{6,7},{8,9},{9,10},{10,11},{11... | collective-permute-start | bytes 3145736 | tf_op jit(solution)/shard_map/ppermute | solution.py:17
  22.7 2.3 copy.26
  25.1 2.9 maximum_bitcast_fusion
  28.0 2.9 maximum_bitcast_fusion.1
  30.9 7.3 %all-gather.7.cloned.1.call-done = bf16[1,512,1024]{2,1,0:T(8,128)(2,1)} async-done(((bf16[1,64,1024]{2,1,0:T(8,128)(2,1)}), bf16[1,512,1024]{2,1,0:T(8,128)(2,1)}) %all-gather.7.cloned.1.call-update) | async-done | bytes 1048592 | tf_op jit(solution)/shard_map/all_gather | solution.py:96
  38.2 25.5 %all-gather.5.cloned.1.call-done = bf16[1,512,1024]{2,1,0:T(8,128)(2,1)} async-done(((bf16[1,64,1024]{2,1,0:T(8,128)(2,1)}), bf16[1,512,1024]{2,1,0:T(8,128)(2,1)}) %all-gather.5.cloned.1.call-update) | async-done | bytes 1048592 | tf_op jit(solution)/shard_map/all_gather | solution.py:95
  65.4 169.8 %while.29 = (s32[]{:T(128)}, bf16[8,512,128]{1,2,0:T(8,128)(2,1)}, bf16[8,512,128]{2,1,0:T(8,128)(2,1)}, f32[8,1024,128]{2,1,0:T(8,128)}, f32[8,1024,128]{2,1,0:...) while((s32[]{:T(128)}, bf16[8,512,128]{1,2,0:T(8,128)(2,1)}, ...), condition=%wide.region_8.9_spmd.clone, body=%wide.region_0.8_spmd.clone.sunk | while | flops 869654016 | bytes 19551504 | solution.py:125
  77.8 2.5 select_reduce_fusion.2
  99.0 2.5 select_reduce_fusion.2
  109.8 2.0 fusion.160
  120.2 2.5 select_reduce_fusion.2
  141.4 2.5 select_reduce_fusion.2
  162.7 2.5 select_reduce_fusion.2
  183.9 2.5 select_reduce_fusion.2
  205.1 2.5 select_reduce_fusion.2
  215.9 2.0 fusion.160
  226.4 2.5 select_reduce_fusion.2
  235.3 4.0 %slice_bitcast_fusion.3 = (f32[8,64,8,128]{3,2,1,0:T(8,128)}, f32[8,64,8,128]{3,2,1,0:T(8,128)S(1)}) fusion(f32[1024,8,128]{2,0,1:T(8,128)} %bitcast.240), kind=kLoop, calls=%fused_computation.130 | loop fusion | bytes 8388608
  248.4 79.4 %psum.23 = f32[8]{0:T(128)} all-reduce(f32[8]{0:T(128)S(1)} %get-tuple-element.149), channel_id=1, replica_groups=mesh['dp'=4,'ctx'=8] {'dp','ctx'}, use_global_device_ids=true, to_apply=%region_11.12 | all-reduce | flops 8 | bytes 64 | tf_op jit(solution)/shard_map/psum | solution.py:152
  331.1 4.3 %all-reduce.3.cloned.1.call-done = (f32[64,1024]{1,0:T(8,128)}, f32[64,1024]{1,0:T(8,128)}) async-done(((f32[64,1024]{1,0:T(8,128)}, f32[64,1024]{1,0:T(8,128)}), (f32[64,1024]{1,0:T(8,128)}, f32[64,1024]{1,0:T(8,128)})) %all-reduce.3.cloned.1.call-update) | async-done | bytes 524304 | tf_op jit(solution)/shard_map/psum | solution.py:147
  335.3 3.8 %gather_fusion = f32[512,1024]{1,0:T(8,128)S(1)} fusion(f32[64,1024]{1,0:T(8,128)} %get-tuple-element.315, s32[1024]{0:T(1024)S(1)} %pad_clamp_fusion), kind=kCustom, calls=%fused_computation | custom fusion | bytes 4196352 | tf_op jit(solution)/shard_map/gather | solution.py:150
  339.2 2.7 gather_fusion.1
  341.8 6.0 %fusion.99 = (bf16[1,512,1024]{2,1,0:T(8,128)(2,1)}, bf16[1,512,1024]{2,1,0:T(8,128)(2,1)}) fusion(f32[512,1024]{1,0:T(8,128)} %gather_fusion.1, f32[512,1024]{1,0:T(8,128)} %collective-permute-done.3, f32[8,64,8,128]{3,2,1,0:T(8,128)} %get-tuple-element.327, pred[512]{0:T(512)(128)(4,1)S(1)} %fusion.108, f32[512,1024]{1,0:T(8,128)S(1)} %gather_fusion, ...), kind=kLoop, calls=%fused_computation.134 | loop fusion | flops 4194304 | bytes 14680576 | tf_op jit(solution)/shard_map/convert_element_type | solution.py:157
  (220 shorter events, 157.1 us)
Async XLA Ops:
  7.2 9.0 %copy-start.3 = (bf16[1,512,1024]{2,1,0:T(8,128)(2,1)S(1)}, bf16[1,512,1024]{2,1,0:T(8,128)(2,1)}, u32[]{:S(2)}) copy-start(bf16[1,512,1024]{2,1,0:T(8,128)(2,1)} %param.18) | copy-start | bytes 3145732
  7.2 31.1 %all-gather.7.cloned.1.call-start = ((), (), s32[]{:S(2)}) async-start(), calls=%async_computation.1 | async-start | bytes 1179648 | tf_op jit(solution)/shard_map/all_gather | solution.py:96
  9.6 54.1 %all-gather.5.cloned.1.call-start = ((), (), s32[]{:S(2)}) async-start(), calls=%async_computation | async-start | bytes 1179648 | tf_op jit(solution)/shard_map/all_gather | solution.py:95
  11.2 324.1 %all-reduce.3.cloned.1.call-start = ((), (), s32[]{:S(2)}) async-start(), calls=%async_computation.2 | async-start | bytes 1048576 | tf_op jit(solution)/shard_map/psum | solution.py:147
  12.8 12.3 %collective-permute-start = (bf16[512,1024]{0,1:T(8,128)(2,1)S(1)}, bf16[512,1024]{0,1:T(8,128)(2,1)}, u32[]{:S(2)}, u32[]{:S(2)}) collective-permute-start(bf16[512,1024]{0,1:T(8,128)(2,1)S(1)} %bitcast.244), channel_id=1, source_target_pairs={{0,1},{1,2},{2,3},{3,4},{4,5},{5,6},{6,7},{8,9},{9,10},{10,11},{11... | collective-permute-start | bytes 3145736 | tf_op jit(solution)/shard_map/ppermute | solution.py:17
  16.7 11.3 %collective-permute-start.1 = (bf16[512,1024]{0,1:T(8,128)(2,1)S(1)}, bf16[512,1024]{0,1:T(8,128)(2,1)}, u32[]{:S(2)}, u32[]{:S(2)}) collective-permute-start(bf16[512,1024]{0,1:T(8,128)(2,1)S(1)} %bitcast.242), channel_id=1, source_target_pairs={{0,1},{1,2},{2,3},{3,4},{4,5},{5,6},{6,7},{8,9},{9,10},{10,11},{11... | collective-permute-start | bytes 3145736 | tf_op jit(solution)/shard_map/ppermute | solution.py:17
  28.0 37.5 %copy-start.2 = (bf16[1,512,1024]{1,2,0:T(8,128)(2,1)S(1)}, bf16[1,512,1024]{1,2,0:T(8,128)(2,1)}, u32[]{:S(2)}) copy-start(bf16[1,512,1024]{1,2,0:T(8,128)(2,1)} %copy.26) | copy-start | bytes 3145732
  28.0 37.5 %copy-start.8 = (f32[8]{0:T(128)S(1)}, f32[8]{0:T(128)}, u32[]{:S(2)}) copy-start(f32[8]{0:T(128)} %param.20) | copy-start | bytes 100
  239.2 3.0 copy-start.1
  240.8 101.0 %collective-permute-start.2 = (f32[512,1024]{1,0:T(8,128)}, f32[512,1024]{1,0:T(8,128)}, u32[]{:S(2)}, u32[]{:S(2)}) collective-permute-start(f32[512,1024]{1,0:T(8,128)} %bitcast.178), channel_id=1, source_target_pairs={{1,0},{2,1},{3,2},{4,3},{5,4},{6,5},{7,6},{9,8},{10,9},{11,10},{12... | collective-permute-start | bytes 6291464 | tf_op jit(solution)/shard_map/ppermute | solution.py:17
  243.9 2.9 copy-start.7
  243.9 3.7 %copy-start.6 = (f32[8,64,128]{2,1,0:T(8,128)S(1)}, f32[8,64,128]{2,1,0:T(8,128)}, u32[]{:S(2)}) copy-start(f32[8,64,128]{2,1,0:T(8,128)} %get-tuple-element.146) | copy-start | bytes 786436
  243.9 83.9 %copy-start.5 = (bf16[8,512,128]{2,1,0:T(8,128)(2,1)S(1)}, bf16[8,512,128]{2,1,0:T(8,128)(2,1)}, u32[]{:S(2)}) copy-start(bf16[8,512,128]{2,1,0:T(8,128)(2,1)} %get-tuple-element.144) | copy-start | bytes 3145732
  245.5 96.3 %collective-permute-start.3 = (f32[512,1024]{1,0:T(8,128)}, f32[512,1024]{1,0:T(8,128)}, u32[]{:S(2)}, u32[]{:S(2)}) collective-permute-start(f32[512,1024]{1,0:T(8,128)} %bitcast.177), channel_id=1, source_target_pairs={{1,0},{2,1},{3,2},{4,3},{5,4},{6,5},{7,6},{9,8},{10,9},{11,10},{12... | collective-permute-start | bytes 6291464 | tf_op jit(solution)/shard_map/ppermute | solution.py:17
  327.8 2.0 copy-start.4
  335.3 3.8 %copy-start = (f32[64,1024]{1,0:T(8,128)S(1)}, f32[64,1024]{1,0:T(8,128)}, u32[]{:S(2)}) copy-start(f32[64,1024]{1,0:T(8,128)} %get-tuple-element.316) | copy-start | bytes 786436
Sparse Core Ops, SparseCore 0:
  9.9 28.2 all-gather.6
  40.1 23.5 all-gather.4
  248.4 86.8 all-reduce.2
where the time goes:
time: 357 us; the launch traced here: 354 us
  matrix products  133 us (37%)
  blocking collectives  79.4 us (22%)
  waiting for transfers between devices  37.1 us (10%)
  local copies, waits for them, and re-layouts  36.4 us (10%)
  other arithmetic  32.7 us (9%)
  between operations  14.7 us (4%)
  starting transfers between devices  10.7 us (3%)
  loops' own time  10 us (3%)
    psum x1, blocking collectives, per_device(): bias_grad = lax.psum(dbias, ('dp', 'ctx'))  79.4 us
    all_gather x1, waiting for transfers between devices, per_device(): lax.all_gather(piece_k, 'ctx', axis=0, tiled=True)  25.5 us
    dot_general x8, matrix products, head_block(): jnp.dot(doh, vb.T, preferred_element_type=jnp.float32) - delta[:, None]  19.7 us
    dot_general x8, matrix products, head_block(): jnp.dot(qh, kb.T, preferred_element_type=jnp.float32) * scale  15.9 us
    unnamed x29, local copies, waits for them, and re-layouts  13.2 us
    dot_general x8, matrix products, head_block(): jnp.dot(wb16, vb, preferred_element_type=jnp.float32)  12.9 us
    dot_general x8, matrix products, head_block(): jnp.dot(wc16, vc, preferred_element_type=jnp.float32)  12.9 us
    dot_general x8, matrix products, head_block(): dvb = jnp.dot(wb16.T, doh, preferred_element_type=jnp.float32)  12.7 us
  transfers between devices with their start and end apart: 7, of which 3 were waited for; matrix products, arithmetic and copies ran while one was open for 8% of the time, Pallas kernels for 0%

commit v1 on v0

--- a/solution.py
+++ b/solution.py
@@ -149,7 +149,8 @@
     source = jnp.clip(qpos // STRIDE * CB + qpos % CB, 0, ncol * CB - 1)
     own_dk = own_dk + jnp.where(flags[:, None], summed_k[source], 0.0)
     own_dv = own_dv + jnp.where(flags[:, None], summed_v[source], 0.0)
-    bias_grad = lax.psum(dbias, ("dp", "ctx"))
+    blocks = lax.all_gather(dbias, ("dp", "ctx"), axis=0, tiled=False)
+    bias_grad = blocks.sum(axis=0)
     return (
         attended[None],
         query_grad[None],

time: 357 us -> 359 us (level)
    psum x1 -> x0, blocking collectives: 79.4 us -> none  [per_device(): bias_grad = lax.psum(dbias, ('dp', 'ctx'))]
    unnamed x0 -> x1, blocking collectives: none -> 75.9 us
    unnamed x29 -> x31, local copies, waits for them, and re-layouts: 13.2 us -> 13.3 us
where the time goes in v1:
time: 359 us; the launch traced here: 356 us
  matrix products  134 us (37%)
  blocking collectives  75.9 us (21%)
  waiting for transfers between devices  39.9 us (11%)
  local copies, waits for them, and re-layouts  36.6 us (10%)
  other arithmetic  33.2 us (9%)
  between operations  14.7 us (4%)
  loops' own time  11 us (3%)
  starting transfers between devices  10.7 us (3%)
    unnamed x1, blocking collectives  75.9 us
    all_gather x1, waiting for transfers between devices, per_device(): lax.all_gather(piece_k, 'ctx', axis=0, tiled=True)  25.5 us
    dot_general x8, matrix products, head_block(): jnp.dot(doh, vb.T, preferred_element_type=jnp.float32) - delta[:, None]  19.7 us
    dot_general x8, matrix products, head_block(): jnp.dot(qh, kb.T, preferred_element_type=jnp.float32) * scale  15.9 us
    unnamed x31, local copies, waits for them, and re-layouts  13.3 us
    dot_general x8, matrix products, head_block(): jnp.dot(wb16, vb, preferred_element_type=jnp.float32)  12.9 us
    dot_general x8, matrix products, head_block(): jnp.dot(wc16, vc, preferred_element_type=jnp.float32)  12.9 us
    dot_general x8, matrix products, head_block(): dvb = jnp.dot(wb16.T, doh, preferred_element_type=jnp.float32)  12.7 us
  transfers between devices with their start and end apart: 7, of which 3 were waited for; matrix products, arithmetic and copies ran while one was open for 8% of the time, Pallas kernels for 0%

profile of v1, /device:TPU:0, one launch (start us, length us, event | category | flops | bytes accessed | tf_op | source)
XLA Modules:
  0.0 356.0 jit_solution(3540969112089438092)
XLA Ops:
  12.8 3.3 collective-permute-start
  16.7 4.6 %collective-permute-start.1 = (bf16[512,1024]{0,1:T(8,128)(2,1)S(1)}, bf16[512,1024]{0,1:T(8,128)(2,1)}, u32[]{:S(2)}, u32[]{:S(2)}) collective-permute-start(bf16[512,1024]{0,1:T(8,128)(2,1)S(1)} %bitcast.242), channel_id=1, source_target_pairs={{0,1},{1,2},{2,3},{3,4},{4,5},{5,6},{6,7},{8,9},{9,10},{10,11},{11... | collective-permute-start | bytes 3145736 | tf_op jit(solution)/shard_map/ppermute | solution.py:17
  22.7 2.3 copy.26
  25.1 2.9 maximum_bitcast_fusion
  28.0 2.9 maximum_bitcast_fusion.1
  30.9 7.4 %all-gather.8.cloned.1.call-done = bf16[1,512,1024]{2,1,0:T(8,128)(2,1)} async-done(((bf16[1,64,1024]{2,1,0:T(8,128)(2,1)}), bf16[1,512,1024]{2,1,0:T(8,128)(2,1)}) %all-gather.8.cloned.1.call-update) | async-done | bytes 1048592 | tf_op jit(solution)/shard_map/all_gather | solution.py:96
  38.2 25.5 %all-gather.6.cloned.1.call-done = bf16[1,512,1024]{2,1,0:T(8,128)(2,1)} async-done(((bf16[1,64,1024]{2,1,0:T(8,128)(2,1)}), bf16[1,512,1024]{2,1,0:T(8,128)(2,1)}) %all-gather.6.cloned.1.call-update) | async-done | bytes 1048592 | tf_op jit(solution)/shard_map/all_gather | solution.py:95
  65.4 171.3 %while.29 = (s32[]{:T(128)}, bf16[8,512,128]{1,2,0:T(8,128)(2,1)}, bf16[8,512,128]{2,1,0:T(8,128)(2,1)}, f32[8,1024,128]{2,1,0:T(8,128)}, f32[8,1024,128]{2,1,0:...) while((s32[]{:T(128)}, bf16[8,512,128]{1,2,0:T(8,128)(2,1)}, ...), condition=%wide.region_8.9_spmd.clone, body=%wide.region_0.8_spmd.clone.sunk | while | flops 869654016 | bytes 19551504 | solution.py:125
  77.8 2.5 select_reduce_fusion.2
  99.3 2.5 select_reduce_fusion.2
  110.2 2.0 fusion.160
  120.7 2.5 select_reduce_fusion.2
  142.1 2.5 select_reduce_fusion.2
  153.0 2.0 fusion.160
  163.5 2.5 select_reduce_fusion.2
  184.9 2.5 select_reduce_fusion.2
  206.3 2.5 select_reduce_fusion.2
  227.8 2.5 select_reduce_fusion.2
  236.8 4.0 %slice_bitcast_fusion.3 = (f32[8,64,8,128]{3,2,1,0:T(8,128)}, f32[8,64,8,128]{3,2,1,0:T(8,128)S(1)}) fusion(f32[1024,8,128]{2,0,1:T(8,128)} %bitcast.240), kind=kLoop, calls=%fused_computation.130 | loop fusion | bytes 8388608
  253.4 75.9 %all-reduce = f32[256]{0:T(256)S(1)} all-reduce(f32[256]{0:T(256)S(1)} %dynamic-update-slice.6), channel_id=4, replica_groups=mesh['dp'=4,'ctx'=8] {'dp','ctx'}, use_global_device_ids=true, to_apply=%add | all-reduce | flops 256 | bytes 2048
  330.0 7.0 %all-reduce.4.cloned.1.call-done = (f32[64,1024]{1,0:T(8,128)}, f32[64,1024]{1,0:T(8,128)}) async-done(((f32[64,1024]{1,0:T(8,128)}, f32[64,1024]{1,0:T(8,128)}), (f32[64,1024]{1,0:T(8,128)}, f32[64,1024]{1,0:T(8,128)})) %all-reduce.4.cloned.1.call-update) | async-done | bytes 524304 | tf_op jit(solution)/shard_map/psum | solution.py:147
  337.0 3.8 %gather_fusion = f32[512,1024]{1,0:T(8,128)S(1)} fusion(f32[64,1024]{1,0:T(8,128)} %get-tuple-element.315, s32[1024]{0:T(1024)S(1)} %pad_clamp_fusion), kind=kCustom, calls=%fused_computation | custom fusion | bytes 4196352 | tf_op jit(solution)/shard_map/gather | solution.py:150
  340.8 2.7 gather_fusion.1
  343.5 6.0 %fusion.99 = (bf16[1,512,1024]{2,1,0:T(8,128)(2,1)}, bf16[1,512,1024]{2,1,0:T(8,128)(2,1)}) fusion(f32[512,1024]{1,0:T(8,128)} %gather_fusion.1, f32[512,1024]{1,0:T(8,128)} %collective-permute-done.3, f32[8,64,8,128]{3,2,1,0:T(8,128)} %get-tuple-element.327, pred[512]{0:T(512)(128)(4,1)S(1)} %fusion.108, f32[512,1024]{1,0:T(8,128)S(1)} %gather_fusion, ...), kind=kLoop, calls=%fused_computation.134 | loop fusion | flops 4194304 | bytes 14680576 | tf_op jit(solution)/shard_map/convert_element_type | solution.py:158
  (224 shorter events, 158.5 us)
Async XLA Ops:
  7.2 9.0 %copy-start.3 = (bf16[1,512,1024]{2,1,0:T(8,128)(2,1)S(1)}, bf16[1,512,1024]{2,1,0:T(8,128)(2,1)}, u32[]{:S(2)}) copy-start(bf16[1,512,1024]{2,1,0:T(8,128)(2,1)} %param.18) | copy-start | bytes 3145732
  7.2 31.1 %all-gather.8.cloned.1.call-start = ((), (), s32[]{:S(2)}) async-start(), calls=%async_computation.1 | async-start | bytes 1179648 | tf_op jit(solution)/shard_map/all_gather | solution.py:96
  9.6 54.1 %all-gather.6.cloned.1.call-start = ((), (), s32[]{:S(2)}) async-start(), calls=%async_computation | async-start | bytes 1179648 | tf_op jit(solution)/shard_map/all_gather | solution.py:95
  11.2 325.8 %all-reduce.4.cloned.1.call-start = ((), (), s32[]{:S(2)}) async-start(), calls=%async_computation.2 | async-start | bytes 1048576 | tf_op jit(solution)/shard_map/psum | solution.py:147
  12.8 12.3 %collective-permute-start = (bf16[512,1024]{0,1:T(8,128)(2,1)S(1)}, bf16[512,1024]{0,1:T(8,128)(2,1)}, u32[]{:S(2)}, u32[]{:S(2)}) collective-permute-start(bf16[512,1024]{0,1:T(8,128)(2,1)S(1)} %bitcast.244), channel_id=1, source_target_pairs={{0,1},{1,2},{2,3},{3,4},{4,5},{5,6},{6,7},{8,9},{9,10},{10,11},{11... | collective-permute-start | bytes 3145736 | tf_op jit(solution)/shard_map/ppermute | solution.py:17
  16.7 11.3 %collective-permute-start.1 = (bf16[512,1024]{0,1:T(8,128)(2,1)S(1)}, bf16[512,1024]{0,1:T(8,128)(2,1)}, u32[]{:S(2)}, u32[]{:S(2)}) collective-permute-start(bf16[512,1024]{0,1:T(8,128)(2,1)S(1)} %bitcast.242), channel_id=1, source_target_pairs={{0,1},{1,2},{2,3},{3,4},{4,5},{5,6},{6,7},{8,9},{9,10},{10,11},{11... | collective-permute-start | bytes 3145736 | tf_op jit(solution)/shard_map/ppermute | solution.py:17
  27.9 37.5 %copy-start.2 = (bf16[1,512,1024]{1,2,0:T(8,128)(2,1)S(1)}, bf16[1,512,1024]{1,2,0:T(8,128)(2,1)}, u32[]{:S(2)}) copy-start(bf16[1,512,1024]{1,2,0:T(8,128)(2,1)} %copy.26) | copy-start | bytes 3145732
  28.0 37.5 %copy-start.8 = (f32[8]{0:T(128)S(1)}, f32[8]{0:T(128)}, u32[]{:S(2)}) copy-start(f32[8]{0:T(128)} %param.20) | copy-start | bytes 100
  240.7 3.0 copy-start.1
  242.3 101.2 %collective-permute-start.2 = (f32[512,1024]{1,0:T(8,128)}, f32[512,1024]{1,0:T(8,128)}, u32[]{:S(2)}, u32[]{:S(2)}) collective-permute-start(f32[512,1024]{1,0:T(8,128)} %bitcast.178), channel_id=1, source_target_pairs={{1,0},{2,1},{3,2},{4,3},{5,4},{6,5},{7,6},{9,8},{10,9},{11,10},{12... | collective-permute-start | bytes 6291464 | tf_op jit(solution)/shard_map/ppermute | solution.py:17
  245.4 2.9 copy-start.7
  245.4 3.7 %copy-start.6 = (f32[8,64,128]{2,1,0:T(8,128)S(1)}, f32[8,64,128]{2,1,0:T(8,128)}, u32[]{:S(2)}) copy-start(f32[8,64,128]{2,1,0:T(8,128)} %get-tuple-element.146) | copy-start | bytes 786436
  245.4 4.5 %copy-start.5 = (bf16[8,512,128]{2,1,0:T(8,128)(2,1)S(1)}, bf16[8,512,128]{2,1,0:T(8,128)(2,1)}, u32[]{:S(2)}) copy-start(bf16[8,512,128]{2,1,0:T(8,128)(2,1)} %get-tuple-element.144) | copy-start | bytes 3145732
  247.0 96.5 %collective-permute-start.3 = (f32[512,1024]{1,0:T(8,128)}, f32[512,1024]{1,0:T(8,128)}, u32[]{:S(2)}, u32[]{:S(2)}) collective-permute-start(f32[512,1024]{1,0:T(8,128)} %bitcast.177), channel_id=1, source_target_pairs={{1,0},{2,1},{3,2},{4,3},{5,4},{6,5},{7,6},{9,8},{10,9},{11,10},{12... | collective-permute-start | bytes 6291464 | tf_op jit(solution)/shard_map/ppermute | solution.py:17
  249.9 2.0 copy-start.4
  337.0 3.8 %copy-start = (f32[64,1024]{1,0:T(8,128)S(1)}, f32[64,1024]{1,0:T(8,128)}, u32[]{:S(2)}) copy-start(f32[64,1024]{1,0:T(8,128)} %get-tuple-element.316) | copy-start | bytes 786436
Sparse Core Ops, SparseCore 0:
  9.9 28.2 all-gather.7
  40.1 23.5 all-gather.5
  250.0 86.9 all-reduce.3
